TPU v7x, 32 devices: a whole 2x2x4 slice. The times are simulated.
32 devices in a mesh: dom: 32 (over z, y, x, core).
Axes of the slice: x: 2, y: 2, z: 4, core: 2. Of those that a mesh axis runs over, the one named last changes fastest.
Arguments:
- features: bfloat16 [16384, 512], P('dom'), may hold values from -6 to 6
- weight: bfloat16 [512, 512], replicated, may hold values from -0.25 to 0.25
- grad_out: bfloat16 [16384, 512], P('dom'), may hold values from -6 to 6
- adjacency: bfloat16 [768, 128, 128], P('dom'), may hold values from -0.25 to 0.25
- tile_row: int32 [32, 24], P('dom'), may hold values from 0 to 3
- tile_src: int32 [32, 24], P('dom'), may hold values from 0 to 7
- tile_count: int32 [32], P('dom'), may hold values from 1 to 24, as said below
- send_tile: int32 [32, 4], P('dom'), may hold values from 0 to 3
- stale_feat: bfloat16 [32, 4, 128, 512], P('dom'), may hold values from -6 to 6
- stale_grad: bfloat16 [32, 4, 128, 512], P('dom'), may hold values from -6 to 6
- blend: float32 [512], replicated, may hold values from 0.2 to 0.8
Outputs:
- output: bfloat16 [16384, 512], P('dom')
- grad_features: bfloat16 [16384, 512], P('dom')
- grad_weight: bfloat16 [512, 512], replicated
Inputs may be any that keep to these rules, and one draw needn't show every extreme that they name: `tile_count`: counts are skewed; some partition holds all 24 entries.
All inputs are finite; a program needn't handle non-finite values.
Results may differ from a plain program's by a relative error of at most 0.0064.
Values may be sent and summed in bfloat16 or wider, within the bound.
A program may use at most 64 MiB of HBM per device.

v0:
```python
import jax
import jax.numpy as jnp
from jax import lax
from jax.sharding import PartitionSpec as P


def partner(x, axis, bit):
    return lax.ppermute(x, axis, [(i, i ^ 1 << bit) for i in range(lax.axis_size(axis))])


def forward_tiles(adjacency, table, row_ids, src_ids, live_count, tiles_dev):

    def forward_add_entry(entry_idx, totals):
        block_in = lax.dynamic_index_in_dim(table, src_ids[entry_idx], 0, keepdims=False)
        adj_tile = lax.dynamic_index_in_dim(adjacency, entry_idx, 0, keepdims=False)
        product = jnp.dot(adj_tile, block_in, preferred_element_type=jnp.float32)
        current = lax.dynamic_index_in_dim(totals, row_ids[entry_idx], 0, keepdims=False)
        return lax.dynamic_update_index_in_dim(totals, current + product, row_ids[entry_idx], 0)

    start = jnp.zeros((tiles_dev, adjacency.shape[1], table.shape[2]), jnp.float32)
    return lax.fori_loop(0, live_count, forward_add_entry, start)


def backward_tiles(adjacency, dz_tiles, row_ids, src_ids, live_count, slots):

    def backward_add_entry(entry_idx, totals):
        block_in = lax.dynamic_index_in_dim(dz_tiles, row_ids[entry_idx], 0, keepdims=False)
        adj_tile = lax.dynamic_index_in_dim(adjacency, entry_idx, 0, keepdims=False)
        product = lax.dot_general(
            adj_tile, block_in, (((0,), (0,)), ((), ())), preferred_element_type=jnp.float32
        )
        current = lax.dynamic_index_in_dim(totals, src_ids[entry_idx], 0, keepdims=False)
        return lax.dynamic_update_index_in_dim(totals, current + product, src_ids[entry_idx], 0)

    start = jnp.zeros((slots, adjacency.shape[1], dz_tiles.shape[2]), jnp.float32)
    return lax.fori_loop(0, live_count, backward_add_entry, start)


def body(
    features,
    weight,
    grad_out,
    adjacency,
    tile_row,
    tile_src,
    tile_count,
    send_tile,
    stale_feat,
    stale_grad,
    blend,
):
    block_size = adjacency.shape[1]
    width_size = features.shape[1]
    tiles_dev = features.shape[0] // block_size
    rounds = send_tile.shape[1]
    nbits = lax.axis_size("dom").bit_length() - 1
    node_tiles = features.reshape(tiles_dev, block_size, width_size)
    row_ids = tile_row[0]
    src_ids = tile_src[0]
    live_count = tile_count[0]
    send_ids = send_tile[0]
    used_blocks = []
    for round_idx in range(rounds):
        outgoing = lax.dynamic_index_in_dim(node_tiles, send_ids[round_idx], 0, keepdims=False)
        arrived = partner(outgoing, "dom", round_idx * nbits // rounds)
        mixed_block = (1.0 - blend) * stale_feat[0, round_idx].astype(
            jnp.float32
        ) + blend * arrived.astype(jnp.float32)
        used_blocks.append(mixed_block.astype(jnp.bfloat16))
    table = jnp.concatenate([node_tiles, jnp.stack(used_blocks, 0)], 0)
    agg_tiles = forward_tiles(adjacency, table, row_ids, src_ids, live_count, tiles_dev).astype(
        jnp.bfloat16
    )
    agg_flat = agg_tiles.reshape(tiles_dev * block_size, width_size)
    pre = jnp.dot(agg_flat, weight, preferred_element_type=jnp.float32)
    sigma = jax.nn.sigmoid(pre)
    output = (pre * sigma).astype(jnp.bfloat16)
    dpre = (grad_out.astype(jnp.float32) * sigma * (1.0 + pre * (1.0 - sigma))).astype(jnp.bfloat16)
    partial_weight = lax.dot_general(
        agg_flat, dpre, (((0,), (0,)), ((), ())), preferred_element_type=jnp.float32
    )
    grad_weight = lax.psum(partial_weight, "dom").astype(jnp.bfloat16)
    dagg = jnp.dot(dpre, weight.T, preferred_element_type=jnp.float32).astype(jnp.bfloat16)
    dz_tiles = dagg.reshape(tiles_dev, block_size, width_size)
    totals = backward_tiles(adjacency, dz_tiles, row_ids, src_ids, live_count, tiles_dev + rounds)
    local_part = totals[:tiles_dev]
    outgoing_grads = totals[tiles_dev:].astype(jnp.bfloat16)
    for round_idx in range(rounds):
        returned = partner(outgoing_grads[round_idx], "dom", round_idx * nbits // rounds)
        corrected = (1.0 - blend) * stale_grad[0, round_idx].astype(
            jnp.float32
        ) + blend * returned.astype(jnp.float32)
        current = lax.dynamic_index_in_dim(local_part, send_ids[round_idx], 0, keepdims=False)
        local_part = lax.dynamic_update_index_in_dim(
            local_part, current + corrected, send_ids[round_idx], 0
        )
    grad_features = local_part.astype(jnp.bfloat16).reshape(tiles_dev * block_size, width_size)
    return (output, grad_features, grad_weight)


def solution(mesh):
    placed = (
        P("dom", None),
        P(),
        P("dom", None),
        P("dom", None, None),
        P("dom", None),
        P("dom", None),
        P("dom"),
        P("dom", None),
        P("dom", None, None, None),
        P("dom", None, None, None),
        P(),
    )
    return jax.shard_map(
        body,
        mesh=mesh,
        in_specs=placed,
        out_specs=(P("dom", None), P("dom", None), P()),
        check_vma=False,
    )
```

profile of v0, /device:TPU:0, one launch (start us, length us, event | category | flops | bytes accessed | tf_op | source)
XLA Modules:
  0.0 407.7 jit_solution(6520869515674289435)
XLA Ops:
  0.7 1.5 fusion.46
  10.0 1.1 dynamic-slice_bitcast_fusion
  11.2 3.1 collective-permute-start.3
  14.3 1.5 collective-permute-start.2
  15.8 1.5 collective-permute-start.1
  17.3 0.7 broadcast_subtract_fusion
  18.0 1.1 constant_dynamic-update-slice_fusion
  19.2 1.6 collective-permute-done.1
  21.0 0.1 broadcast_in_dim.43
  21.2 27.5 %while.20 = (s32[]{:T(128)}, f32[4,128,512]{2,1,0:T(8,128)S(1)}, s32[]{:T(128)}, s32[24]{0:T(128)S(1)}, bf16[24,128,128]{2,1,0:T(8,128)(2,1)}, /*index=5*/s32[24...) while((s32[]{:T(128)}, f32[4,128,512]{2,1,0:T(8,128)S(1)}, ...), condition=%wide.region_1.2_spmd, body=%wide.region_0.1_spmd.sunk | while | flops 16842764 | bytes 1212683 | solution.py:21
  21.9 0.6 dynamic_slice.110
  24.4 0.6 dynamic_slice.111
  27.0 0.9 fusion.62
  28.6 0.6 dynamic_slice.110
  31.1 0.6 dynamic_slice.111
  33.7 0.9 fusion.62
  35.3 0.6 dynamic_slice.110
  37.8 0.6 dynamic_slice.111
  40.4 0.9 fusion.62
  42.0 0.6 dynamic_slice.110
  44.5 0.6 dynamic_slice.111
  47.1 0.9 fusion.62
  48.8 1.6 multiply_convert_fusion
  50.4 1.4 fusion.47
  51.9 0.5 convolution_convert_fusion
  52.3 0.2 broadcast_in_dim.44
  52.6 27.6 %while.21 = (s32[]{:T(128)}, f32[8,128,512]{2,1,0:T(8,128)S(1)}, s32[]{:T(128)}, s32[24]{0:T(128)S(1)}, bf16[24,128,128]{2,1,0:T(8,128)(2,1)}, /*index=5*/s32[24...) while((s32[]{:T(128)}, f32[8,128,512]{2,1,0:T(8,128)S(1)}, ...), condition=%wide.region_3.4_spmd, body=%wide.region_2.3_spmd.sunk | while | flops 16842764 | bytes 1212683 | solution.py:36
  53.3 0.6 dynamic_slice.115
  55.8 0.6 dynamic_slice.116
  58.4 1.0 fusion.65
  60.0 0.6 dynamic_slice.115
  62.5 0.6 dynamic_slice.116
  65.1 1.0 fusion.65
  66.7 0.6 dynamic_slice.115
  69.3 0.6 dynamic_slice.116
  71.8 1.0 fusion.65
  73.5 0.6 dynamic_slice.115
  76.0 0.6 dynamic_slice.116
  78.6 1.0 fusion.65
  80.2 0.1 convert.11
  80.4 0.7 slice_bitcast_fusion
  81.1 318.1 %all-reduce.1 = bf16[512,512]{1,0:T(8,128)(2,1)} all-reduce(f32[512,512]{1,0:T(8,128)} %fusion.47), channel_id=1, replica_groups=mesh['dom'=32] {'dom'}, use_global_device_ids=true, to_apply=%region_4.5 | all-reduce | flops 262144 | bytes 1572864 | tf_op jit(solution)/shard_map/psum | solution.py:82
  399.2 0.1 slice.77
  399.2 1.0 collective-permute-start.7
  400.2 1.3 collective-permute-start.6
  401.5 0.7 collective-permute-start.5
  402.4 4.1 %collective-permute-done.5 = bf16[128,512]{1,0:T(8,128)(2,1)S(1)} collective-permute-done((bf16[128,512]{1,0:T(8,128)(2,1)S(1)}, bf16[128,512]{1,0:T(8,128)(2,1)S(1)}, u32[]{:S(2)}, u32[]{:S(2)}) %collective-permute-start.5) | collective-permute-done | bytes 131104 | tf_op jit(solution)/shard_map/ppermute | solution.py:8
  406.8 0.9 convert_element_type.139
  (45 shorter events, 0.9 us)
Async XLA Ops:
  0.6 48.2 %copy-start = (bf16[512,512]{1,0:T(8,128)(2,1)S(1)}, bf16[512,512]{1,0:T(8,128)(2,1)}, u32[]{:S(2)}) copy-start(bf16[512,512]{1,0:T(8,128)(2,1)} %param.16) | copy-start | bytes 1572868
  0.6 18.5 %copy-start.3 = (f32[512]{0:T(512)S(1)}, f32[512]{0:T(512)}, u32[]{:S(2)}) copy-start(f32[512]{0:T(512)} %param.25) | copy-start | bytes 6148
  0.7 18.5 %copy-start.1 = (bf16[1,4,128,512]{3,2,1,0:T(8,128)(2,1)S(1)}, bf16[1,4,128,512]{3,2,1,0:T(8,128)(2,1)}, u32[]{:S(2)}) copy-start(bf16[1,4,128,512]{3,2,1,0:T(8,128)(2,1)} %param.23) | copy-start | bytes 1572868
  11.2 10.0 %copy-start.6 = (s32[1,24]{1,0:T(1,128)S(1)}, s32[1,24]{1,0:T(1,128)}, u32[]{:S(2)}) copy-start(s32[1,24]{1,0:T(1,128)} %param.19) | copy-start | bytes 292
  11.2 10.0 %copy-start.7 = (s32[1,24]{1,0:T(1,128)S(1)}, s32[1,24]{1,0:T(1,128)}, u32[]{:S(2)}) copy-start(s32[1,24]{1,0:T(1,128)} %param.20) | copy-start | bytes 292
  11.2 9.7 %collective-permute-start.3 = (bf16[128,512]{1,0:T(8,128)(2,1)S(1)}, bf16[128,512]{1,0:T(8,128)(2,1)S(1)}, u32[]{:S(2)}, u32[]{:S(2)}) collective-permute-start(bf16[128,512]{1,0:T(8,128)(2,1)S(1)} %get-tuple-element.115), channel_id=1, source_target_pairs={{0,8},{1,9},{2,10},{3,11},{4,12},{5,13},{6,14},{7,15},{8,0},{9,1},... | collective-permute-start | bytes 393224 | tf_op jit(solution)/shard_map/ppermute | solution.py:8
  14.3 6.5 %collective-permute-start.2 = (bf16[128,512]{1,0:T(8,128)(2,1)S(1)}, bf16[128,512]{1,0:T(8,128)(2,1)S(1)}, u32[]{:S(2)}, u32[]{:S(2)}) collective-permute-start(bf16[128,512]{1,0:T(8,128)(2,1)S(1)} %get-tuple-element.116), channel_id=1, source_target_pairs={{0,4},{1,5},{2,6},{3,7},{4,0},{5,1},{6,2},{7,3},{8,12},{9,13},{10,... | collective-permute-start | bytes 393224 | tf_op jit(solution)/shard_map/ppermute | solution.py:8
  15.8 5.0 %collective-permute-start.1 = (bf16[128,512]{1,0:T(8,128)(2,1)S(1)}, bf16[128,512]{1,0:T(8,128)(2,1)S(1)}, u32[]{:S(2)}, u32[]{:S(2)}) collective-permute-start(bf16[128,512]{1,0:T(8,128)(2,1)S(1)} %get-tuple-element.117), channel_id=1, source_target_pairs={{0,2},{1,3},{2,0},{3,1},{4,6},{5,7},{6,4},{7,5},{8,10},{9,11},{10,... | collective-permute-start | bytes 393224 | tf_op jit(solution)/shard_map/ppermute | solution.py:8
  17.3 1.8 collective-permute-start
  21.2 27.6 %copy-start.5 = (bf16[512,512]{1,0:T(8,128)(2,1)S(1)}, bf16[512,512]{1,0:T(8,128)(2,1)}, u32[]{:S(2)}) copy-start(bf16[512,512]{1,0:T(8,128)(2,1)} %param.17) | copy-start | bytes 1572868
  81.1 321.2 %copy-start.2 = (bf16[1,4,128,512]{3,2,1,0:T(8,128)(2,1)S(1)}, bf16[1,4,128,512]{3,2,1,0:T(8,128)(2,1)}, u32[]{:S(2)}) copy-start(bf16[1,4,128,512]{3,2,1,0:T(8,128)(2,1)} %param.24) | copy-start | bytes 1572868
  81.1 321.2 %collective-permute-start.4 = (bf16[128,512]{1,0:T(8,128)(2,1)}, bf16[128,512]{1,0:T(8,128)(2,1)S(1)}, u32[]{:S(2)}, u32[]{:S(2)}) collective-permute-start(bf16[128,512]{1,0:T(8,128)(2,1)} %get-tuple-element.112), channel_id=1, source_target_pairs={{0,1},{1,0},{2,3},{3,2},{4,5},{5,4},{6,7},{7,6},{8,9},{9,8},{10,11... | collective-permute-start | bytes 393224 | tf_op jit(solution)/shard_map/ppermute | solution.py:8
  399.2 2.4 copy-start.4
  399.2 7.5 %collective-permute-start.7 = (bf16[128,512]{1,0:T(8,128)(2,1)S(1)}, bf16[128,512]{1,0:T(8,128)(2,1)S(1)}, u32[]{:S(2)}, u32[]{:S(2)}) collective-permute-start(bf16[128,512]{1,0:T(8,128)(2,1)S(1)} %get-tuple-element.109), channel_id=1, source_target_pairs={{0,8},{1,9},{2,10},{3,11},{4,12},{5,13},{6,14},{7,15},{8,0},{9,1},... | collective-permute-start | bytes 393224 | tf_op jit(solution)/shard_map/ppermute | solution.py:8
  400.2 6.4 %collective-permute-start.6 = (bf16[128,512]{1,0:T(8,128)(2,1)S(1)}, bf16[128,512]{1,0:T(8,128)(2,1)S(1)}, u32[]{:S(2)}, u32[]{:S(2)}) collective-permute-start(bf16[128,512]{1,0:T(8,128)(2,1)S(1)} %get-tuple-element.110), channel_id=1, source_target_pairs={{0,4},{1,5},{2,6},{3,7},{4,0},{5,1},{6,2},{7,3},{8,12},{9,13},{10,... | collective-permute-start | bytes 393224 | tf_op jit(solution)/shard_map/ppermute | solution.py:8
  401.5 5.0 %collective-permute-start.5 = (bf16[128,512]{1,0:T(8,128)(2,1)S(1)}, bf16[128,512]{1,0:T(8,128)(2,1)S(1)}, u32[]{:S(2)}, u32[]{:S(2)}) collective-permute-start(bf16[128,512]{1,0:T(8,128)(2,1)S(1)} %copy-done.4), channel_id=1, source_target_pairs={{0,2},{1,3},{2,0},{3,1},{4,6},{5,7},{6,4},{7,5},{8,10},{9,11},{10,... | collective-permute-start | bytes 393224 | tf_op jit(solution)/shard_map/ppermute | solution.py:8
where the time goes:
time: 414 us; the launch traced here: 408 us
  blocking collectives  318 us (77%)
  loops' own time  37.9 us (9%)
  local copies, waits for them, and re-layouts  14.6 us (4%)
  matrix products  11.1 us (3%)
  starting transfers between devices  9.12 us (2%)
  between operations  8.82 us (2%)
  waiting for transfers between devices  5.76 us (1%)
    psum x1, blocking collectives, body(): grad_weight = lax.psum(partial_weight, 'dom').astype(jnp.bfloat16)  318 us
    another operation x1, loops' own time, forward_tiles(): return lax.fori_loop(0, live_count, forward_add_entry, start)  19 us
    another operation x1, loops' own time, backward_tiles(): return lax.fori_loop(0, live_count, backward_add_entry, start)  18.9 us
    ppermute x8, starting transfers between devices, partner(): lax.ppermute(x, axis, [(i, i ^ 1 << bit) for i in range(lax.axis_size(axi...  9.12 us
  transfers between devices with their start and end apart: 8, of which 2 were waited for; matrix products, arithmetic and copies ran while one was open for 1% of the time, Pallas kernels for 0%

commit v1 on v0

v1 whole, which is shorter than its diff:
```python
import functools

import jax
import jax.numpy as jnp
from jax import lax
from jax.experimental import pallas as pl
from jax.experimental.pallas import tpu as pltpu
from jax.sharding import PartitionSpec as P

MESH = pl.DeviceIdType.MESH
F32 = jnp.float32
BF16 = jnp.bfloat16


def bit_of(i, b):
    return lax.rem(lax.div(i, 1 << b), 2)


def flip(i, mask):
    out = i
    for b in range(mask.bit_length()):
        if mask >> b & 1:
            out = out + (1 - 2 * bit_of(i, b)) * (1 << b)
    return out


class Sems:
    def __init__(self, send, recv):
        self.send, self.recv, self.next = send, recv, 0

    def take(self):
        self.next += 1
        return self.next - 1


def names_and_shapes(tiles, block, width, entries, rounds, n_extra):
    nodes = tiles * block
    half, quarter, piece = width // 2, width // 8, width // 32
    v = pltpu.VMEM
    return dict(
        feat=v((tiles, block, width), BF16),
        wgt=v((width, width), BF16),
        gout=v((nodes, width), BF16),
        adj=v((entries, block, block), BF16),
        sfeat=v((rounds, block, width), BF16),
        sgrad=v((rounds, block, width), BF16),
        fsend=v((rounds, block, width), BF16),
        frecv=v((rounds, block, width), BF16),
        used=v((rounds, block, width), BF16),
        chain=v((entries + 1, block, block), F32),
        dense=v((nodes, (tiles + rounds) * block), BF16),
        part=v((nodes, width), F32),
        agg=v((nodes, width), BF16),
        outv=v((nodes, width), BF16),
        dpre=v((nodes, width), BF16),
        dagg=v((nodes, width), BF16),
        back=v((nodes, width), F32),
        gsend=v((rounds, block, width), BF16),
        grecv=v((rounds, block, width), BF16),
        gfeat=v((nodes, width), BF16),
        s0send=v((half, width), BF16),
        s0recv=v((half, width), BF16),
        acc=v((half, width), F32),
        s1send=v((half, width), BF16),
        s1recv=v((3, quarter, width), BF16),
        s2send=v((3, piece, width), BF16),
        s2recv=v((3, piece, width), BF16),
        xbuf=v((max(n_extra, 1), 4, piece, width), BF16),
        gw=v((width, width), BF16),
        lsem=pltpu.SemaphoreType.DMA((16,)),
        ssem=pltpu.SemaphoreType.DMA((96,)),
        rsem=pltpu.SemaphoreType.DMA((96,)),
    )


def kernel(names, nbits, *refs):
    (features, weight, grad_out, adjacency, stale_feat, stale_grad, blend,
     tile_row, tile_src, tile_count, send_tile, out_hbm, gf_hbm, gw_hbm) = refs[:14]
    s = dict(zip(names, refs[14:]))
    tiles, block, width = s["feat"].shape
    rounds = s["fsend"].shape[0]
    entries = s["adj"].shape[0]
    nodes = tiles * block
    half, quarter, piece = width // 2, width // 8, width // 32
    me = lax.axis_index("dom")
    sems = Sems(s["ssem"], s["rsem"])
    pending = []

    def remote(src, dst, mask):
        i = sems.take()
        c = pltpu.make_async_remote_copy(
            src_ref=src, dst_ref=dst, send_sem=s["ssem"].at[i], recv_sem=s["rsem"].at[i],
            device_id=(flip(me, mask),), device_id_type=MESH)
        c.start()
        pending.append(c)
        return c

    loads = {}
    for i, (src, name) in enumerate((
            (features, "feat"), (adjacency, "adj"), (stale_feat.at[0], "sfeat"),
            (weight, "wgt"), (grad_out, "gout"), (stale_grad.at[0], "sgrad"))):
        loads[name] = pltpu.make_async_copy(src, s[name], s["lsem"].at[i])
        loads[name].start()

    round_mask = [1 << (r * nbits // rounds) for r in range(rounds)]
    extra = []
    b = 5
    while b < nbits:
        extra.append((b, min(2, nbits - b)))
        b += 2
    peers = {1} | {k << 1 for k in (1, 2, 3)} | {k << 3 for k in (1, 2, 3)} | set(round_mask)
    for lo, nb in extra:
        peers |= {k << lo for k in range(1, 1 << nb)}
    barrier = pltpu.get_barrier_semaphore()
    for m in sorted(peers):
        pl.semaphore_signal(barrier, inc=1, device_id=(flip(me, m),), device_id_type=MESH)

    loads["feat"].wait()
    for r in range(rounds):
        s["fsend"][r] = s["feat"][send_tile[0, r]]
    pl.semaphore_wait(barrier, len(peers))
    fcopies = [remote(s["fsend"].at[r], s["frecv"].at[r], round_mask[r]) for r in range(rounds)]

    live = tile_count[0]
    cells = tiles + rounds
    keys = [jnp.where(e < live, tile_row[0, e] * cells + tile_src[0, e], -1 - e) for e in range(entries)]
    loads["adj"].wait()
    s["chain"][0] = jnp.zeros((block, block), F32)
    for e in range(entries):
        prev = jnp.int32(0)
        for f in range(e):
            prev = jnp.where(keys[f] == keys[e], f + 1, prev)
        s["chain"][e + 1] = s["chain"][prev] + s["adj"][e].astype(F32)
    for t in range(tiles):
        for c in range(cells):
            last = jnp.int32(0)
            for e in range(entries):
                last = jnp.where(keys[e] == t * cells + c, e + 1, last)
            s["dense"][t * block:(t + 1) * block, c * block:(c + 1) * block] = s["chain"][last].astype(BF16)

    mix = blend[...]
    keep = 1.0 - mix
    s["part"][...] = jnp.dot(s["dense"][:, :nodes], s["feat"][...].reshape(nodes, width),
                             preferred_element_type=F32)
    loads["sfeat"].wait()
    for r in range(rounds):
        fcopies[r].wait_recv()
        s["used"][r] = (keep * s["sfeat"][r].astype(F32) + mix * s["frecv"][r].astype(F32)).astype(BF16)
    loads["wgt"].wait()
    loads["gout"].wait()
    for t in range(tiles):
        rows = slice(t * block, (t + 1) * block)
        agg = (s["part"][rows, :] + jnp.dot(
            s["dense"][rows, nodes:], s["used"][...].reshape(rounds * block, width),
            preferred_element_type=F32)).astype(BF16)
        s["agg"][rows, :] = agg
        pre = jnp.dot(agg, s["wgt"][...], preferred_element_type=F32)
        sigma = jax.nn.sigmoid(pre)
        s["outv"][rows, :] = (pre * sigma).astype(BF16)
        s["dpre"][rows, :] = (s["gout"][rows, :].astype(F32) * sigma * (1.0 + pre * (1.0 - sigma))).astype(BF16)
    out_copy = pltpu.make_async_copy(s["outv"], out_hbm, s["lsem"].at[8])
    out_copy.start()

    j0 = bit_of(me, 0)
    j1 = lax.rem(lax.div(me, 2), 4)
    j2 = lax.rem(lax.div(me, 8), 4)

    def half_product(h):
        cols = pl.ds(pl.multiple_of(h * half, half), half)
        return lax.dot_general(s["agg"][:, cols], s["dpre"][...], (((0,), (0,)), ((), ())),
                               preferred_element_type=F32)

    def quarter_rows(k):
        return pl.ds(pl.multiple_of(flip(j1, k) * quarter, quarter), quarter)

    def piece_rows(k, base=0):
        return pl.ds(pl.multiple_of(base + flip(j2, k) * piece, piece), piece)

    s["s0send"][...] = half_product(1 - j0).astype(BF16)
    order1 = (3, 1, 2, 0)
    core = {}
    for k in order1:
        core[k] = remote(s["s0send"].at[quarter_rows(k)], s["s0recv"].at[quarter_rows(k)], 1)
    s["acc"][...] = half_product(j0)
    plane = {}
    for k in order1:
        core[k].wait_recv()
        total = s["acc"][quarter_rows(k), :] + s["s0recv"][quarter_rows(k), :].astype(F32)
        if k == 0:
            s["acc"][quarter_rows(0), :] = total
            continue
        s["s1send"][quarter_rows(k), :] = total.astype(BF16)
        for kz in (3, 2, 1, 0):
            plane[k, kz] = remote(s["s1send"].at[piece_rows(kz, flip(j1, k) * quarter)],
                                  s["s1recv"].at[k - 1, piece_rows(kz)], k << 1)

    s["dagg"][...] = lax.dot_general(s["dpre"][...], s["wgt"][...], (((1,), (1,)), ((), ())),
                                     preferred_element_type=F32).astype(BF16)
    s["gsend"][...] = lax.dot_general(s["dense"][:, nodes:], s["dagg"][...], (((0,), (0,)), ((), ())),
                                      preferred_element_type=F32).astype(BF16).reshape(rounds, block, width)
    gcopies = {}
    late = [r for r in range(rounds) if round_mask[r] in (2, 4)]
    for r in range(rounds):
        if r not in late:
            gcopies[r] = remote(s["gsend"].at[r], s["grecv"].at[r], round_mask[r])
    s["back"][...] = lax.dot_general(s["dense"][:, :nodes], s["dagg"][...], (((0,), (0,)), ((), ())),
                                     preferred_element_type=F32)

    line = {}
    for kz in (3, 2, 1, 0):
        total = s["acc"][piece_rows(kz, j1 * quarter), :]
        for k in (1, 2, 3):
            plane[k, kz].wait_recv()
            total = total + s["s1recv"][k - 1, piece_rows(kz), :].astype(F32)
        if kz:
            s["s2send"][kz - 1] = total.astype(BF16)
            line[kz] = remote(s["s2send"].at[kz - 1], s["s2recv"].at[kz - 1], kz << 3)
    for r in late:
        gcopies[r] = remote(s["gsend"].at[r], s["grecv"].at[r], round_mask[r])
    for kz in (1, 2, 3):
        line[kz].wait_recv()
        total = total + s["s2recv"][kz - 1].astype(F32)
    for g, (lo, nb) in enumerate(extra):
        size = 1 << nb
        jx = lax.rem(lax.div(me, 1 << lo), size)
        s["xbuf"][g, pl.ds(jx, 1)] = total.astype(BF16)[None]
        swaps = [remote(s["xbuf"].at[g, jx], s["xbuf"].at[g, jx], k << lo) for k in range(1, size)]
        for c in swaps:
            c.wait_recv()
        total = s["xbuf"][g, 0].astype(F32)
        for x in range(1, size):
            total = total + s["xbuf"][g, x].astype(F32)

    def gw_rows(kc, kp, kz):
        at = flip(j0, kc) * half + flip(j1, kp) * quarter + flip(j2, kz) * piece
        return pl.ds(pl.multiple_of(at, piece), piece)

    arrivals = {}

    def forward(kc, kp, kz, level):
        ref = s["gw"].at[gw_rows(kc, kp, kz)]
        if level > 2:
            for k in (3, 2, 1):
                arrivals[kc, kp, k] = remote(ref, ref, k << 3)
        if level > 1:
            for k in (3, 1, 2):
                arrivals[kc, k, kz] = remote(ref, ref, k << 1)
        arrivals[1, kp, kz] = remote(ref, ref, 1)

    s["gw"][gw_rows(0, 0, 0), :] = total.astype(BF16)
    forward(0, 0, 0, 3)

    loads["sgrad"].wait()
    hot = [[jnp.where(send_tile[0, r] == t, 1.0, 0.0).astype(F32) for r in range(rounds)] for t in range(tiles)]
    for r in range(rounds):
        gcopies[r].wait_recv()
        corrected = keep * s["sgrad"][r].astype(F32) + mix * s["grecv"][r].astype(F32)
        for t in range(tiles):
            rows = slice(t * block, (t + 1) * block)
            s["back"][rows, :] = s["back"][rows, :] + hot[t][r] * corrected
    s["gfeat"][...] = s["back"][...].astype(BF16)
    gf_copy = pltpu.make_async_copy(s["gfeat"], gf_hbm, s["lsem"].at[9])
    gf_copy.start()

    for kz in (1, 2, 3):
        arrivals[0, 0, kz].wait_recv()
        forward(0, 0, kz, 2)
    for kz in (0, 1, 2, 3):
        for kp in (1, 2, 3):
            arrivals[0, kp, kz].wait_recv()
            forward(0, kp, kz, 1)
    for kz in range(4):
        for kp in range(4):
            arrivals[1, kp, kz].wait_recv()
    gw_copy = pltpu.make_async_copy(s["gw"], gw_hbm, s["lsem"].at[10])
    gw_copy.start()
    for c in pending:
        c.wait_send()
    out_copy.wait()
    gf_copy.wait()
    gw_copy.wait()


def body(nbits, features, weight, grad_out, adjacency, tile_row, tile_src, tile_count,
         send_tile, stale_feat, stale_grad, blend):
    nodes, width = features.shape
    entries, block = adjacency.shape[:2]
    rounds = send_tile.shape[1]
    tiles = nodes // block
    n_extra = (max(nbits - 5, 0) + 1) // 2
    scratch = names_and_shapes(tiles, block, width, entries, rounds, n_extra)
    hbm = pl.BlockSpec(memory_space=pl.ANY)
    smem = pl.BlockSpec(memory_space=pltpu.SMEM)
    vmem = pl.BlockSpec(memory_space=pltpu.VMEM)
    out, gf, gw = pl.pallas_call(
        functools.partial(kernel, tuple(scratch), nbits),
        name="layer",
        out_shape=(jax.ShapeDtypeStruct((nodes, width), BF16),
                   jax.ShapeDtypeStruct((nodes, width), BF16),
                   jax.ShapeDtypeStruct((width, width), BF16)),
        in_specs=[hbm] * 6 + [vmem] + [smem] * 4,
        out_specs=(hbm, hbm, hbm),
        scratch_shapes=list(scratch.values()),
        compiler_params=pltpu.CompilerParams(collective_id=0, has_side_effects=True,
                                             vmem_limit_bytes=48 * 1024 * 1024),
    )(features.reshape(tiles, block, width), weight, grad_out, adjacency, stale_feat, stale_grad,
      blend.reshape(1, width), tile_row, tile_src, tile_count, send_tile)
    return out, gf, gw


def solution(mesh):
    nbits = mesh.shape["dom"].bit_length() - 1
    placed = (
        P("dom", None), P(), P("dom", None), P("dom", None, None), P("dom", None), P("dom", None),
        P("dom"), P("dom", None), P("dom", None, None, None), P("dom", None, None, None), P(),
    )
    return jax.shard_map(
        functools.partial(body, nbits),
        mesh=mesh,
        in_specs=placed,
        out_specs=(P("dom", None), P("dom", None), P()),
        check_vma=False,
    )
```

time: 414 us -> 42 us (0.10); the launches traced: 408 us -> 41.6 us
  blocking collectives: 318 us -> 0 us
  loops' own time: 37.9 us -> 0 us
  Pallas kernels: 0 us -> 30.9 us
  matrix products: 11.1 us -> 0 us
  starting transfers between devices: 9.12 us -> 0 us
  between operations: 8.82 us -> 1.33 us
  waiting for transfers between devices: 5.76 us -> 0 us
  local copies, waits for them, and re-layouts: 14.6 us -> 9.39 us
    psum x1 -> x0, blocking collectives: 318 us -> none  [body(): grad_weight = lax.psum(partial_weight, 'dom').astype(jnp.bfloat16)]
    another operation x2 -> x0, loops' own time: 37.9 us -> none  [the longest x1 19 us: forward_tiles(): return lax.fori_loop(0, live_count, forward_add_entry, start)]
    pallas_call x0 -> x1, Pallas kernels: none -> 30.9 us  [body(): pl.pallas_call(functools.partial(kernel, tuple(scratch), nbits), name='la...]
    dot_general x11 -> x0, matrix products: 11.1 us -> none  [the longest x4 3.89 us: backward_add_entry(): lax.dot_general(adj_tile, block_in, (((0,), (0,)), ((), ())), preferred_e...]
    dynamic_slice x28 -> x0, local copies, waits for them, and re-layouts: 9.71 us -> none  [the longest x4 2.36 us: forward_add_entry(): src_ids[entry_idx]]
    ppermute x8 -> x0, starting transfers between devices: 9.12 us -> none  [partner(): lax.ppermute(x, axis, [(i, i ^ 1 << bit) for i in range(lax.axis_size(axi...]
    unnamed x17 -> x23, local copies, waits for them, and re-layouts: 1.12 us -> 9.39 us
    ppermute x8 -> x0, waiting for transfers between devices: 5.76 us -> none  [partner(): lax.ppermute(x, axis, [(i, i ^ 1 << bit) for i in range(lax.axis_size(axi...]
  transfers between devices with their start and end apart: 8 -> 0, of which waited for: 2 -> 0; matrix products, arithmetic and copies ran while one was open for 1% -> 0% of each run, Pallas kernels for 0% -> 0%
where the time goes in v1:
time: 42 us; the launch traced here: 41.6 us
  Pallas kernels  30.9 us (74%)
  local copies, waits for them, and re-layouts  9.39 us (22%)
  between operations  1.33 us (3%)
    pallas_call x1, Pallas kernels, body(): pl.pallas_call(functools.partial(kernel, tuple(scratch), nbits), name='la...  30.9 us
    unnamed x23, local copies, waits for them, and re-layouts  9.39 us

profile of v1, /device:TPU:0, one launch (start us, length us, event | category | flops | bytes accessed | tf_op | source)
XLA Modules:
  0.0 41.6 jit_solution(18339130971206102413)
XLA Ops:
  1.3 0.0 copy-start.6
  1.3 0.0 copy-start.7
  1.3 0.0 copy-start.8
  1.3 0.0 copy-start.9
  1.3 0.6 %copy-done.6 = f32[512]{0:T(512)S(1)} copy-done((f32[512]{0:T(512)S(1)}, f32[512]{0:T(512)}, u32[]{:S(2)}) %copy-start.6) | copy-done | bytes 2072
  2.0 0.0 copy-done.7
  2.0 0.0 copy-done.8
  2.0 0.0 copy-done.9
  2.0 0.0 copy-start
  2.0 1.1 %copy-done = bf16[24,128,128]{2,1,0:T(8,128)(2,1)S(1)} copy-done((bf16[24,128,128]{2,1,0:T(8,128)(2,1)S(1)}, bf16[24,128,128]{2,1,0:T(8,128)(2,1)}, u32[]{:S(2)}) %copy-start) | copy-done | bytes 786456
  3.1 0.0 copy-start.1
  3.1 1.0 %copy-done.1 = bf16[512,512]{1,0:T(8,128)(2,1)S(1)} copy-done((bf16[512,512]{1,0:T(8,128)(2,1)S(1)}, bf16[512,512]{1,0:T(8,128)(2,1)}, u32[]{:S(2)}) %copy-start.1) | copy-done | bytes 524312
  4.2 0.0 copy-start.2
  4.2 1.0 %copy-done.2 = bf16[512,512]{1,0:T(8,128)(2,1)S(1)} copy-done((bf16[512,512]{1,0:T(8,128)(2,1)S(1)}, bf16[512,512]{1,0:T(8,128)(2,1)}, u32[]{:S(2)}) %copy-start.2) | copy-done | bytes 524312
  5.2 0.0 copy-start.3
  5.2 1.0 %copy-done.3 = bf16[512,512]{1,0:T(8,128)(2,1)S(1)} copy-done((bf16[512,512]{1,0:T(8,128)(2,1)S(1)}, bf16[512,512]{1,0:T(8,128)(2,1)}, u32[]{:S(2)}) %copy-start.3) | copy-done | bytes 524312
  6.2 0.0 copy-start.4
  6.2 1.0 %copy-done.4 = bf16[1,4,128,512]{3,2,1,0:T(8,128)(2,1)S(1)} copy-done((bf16[1,4,128,512]{3,2,1,0:T(8,128)(2,1)S(1)}, bf16[1,4,128,512]{3,2,1,0:T(8,128)(2,1)}, u32[]{:S(2)}) %copy-start.4) | copy-done | bytes 524312
  7.3 0.0 copy-start.5
  7.3 1.0 %copy-done.5 = bf16[1,4,128,512]{3,2,1,0:T(8,128)(2,1)S(1)} copy-done((bf16[1,4,128,512]{3,2,1,0:T(8,128)(2,1)S(1)}, bf16[1,4,128,512]{3,2,1,0:T(8,128)(2,1)}, u32[]{:S(2)}) %copy-start.5) | copy-done | bytes 524312
  8.3 30.9 %layer.1 = (bf16[512,512]{1,0:T(8,128)(2,1)S(1)}, bf16[512,512]{1,0:T(8,128)(2,1)S(1)}, bf16[512,512]{1,0:T(8,128)(2,1)S(1)}) custom-call(bf16[4,128,512]{2,1,0:T(8,128)(2,1)S(1)} %bitcast.2, bf16[512,512]{1,0:T(8,128)(2,1)S(1)} %copy-done.2, bf16[512,512]{1,0:T(8,128)(2,1)S(1)} %copy-done.3, bf16[24,128,128]{2,1,0:T(8,128)(2,1)S(1)} %copy-done, ...), custom_call_target="tpu_custom_call" | custom-call | tf_op jit(solution)/shard_map/layer/pallas_call | solution.py:295
  39.2 0.8 %copy.18 = bf16[512,512]{1,0:T(8,128)(2,1)} copy(bf16[512,512]{1,0:T(8,128)(2,1)S(1)} %get-tuple-element.6) | data formatting | bytes 1048576
  40.0 0.8 %copy.19 = bf16[512,512]{1,0:T(8,128)(2,1)} copy(bf16[512,512]{1,0:T(8,128)(2,1)S(1)} %get-tuple-element.7) | data formatting | bytes 1048576
  40.8 0.8 %copy.20 = bf16[512,512]{1,0:T(8,128)(2,1)} copy(bf16[512,512]{1,0:T(8,128)(2,1)S(1)} %get-tuple-element.8) | data formatting | bytes 1048576
Async XLA Ops:
  1.3 0.7 %copy-start.6 = (f32[512]{0:T(512)S(1)}, f32[512]{0:T(512)}, u32[]{:S(2)}) copy-start(f32[512]{0:T(512)} %param.21) | copy-start | bytes 6148
  1.3 0.7 %copy-start.7 = (s32[1,24]{1,0:T(1,128)S(1)}, s32[1,24]{1,0:T(1,128)}, u32[]{:S(2)}) copy-start(s32[1,24]{1,0:T(1,128)} %refs_7_.1) | copy-start | bytes 292
  1.3 0.7 %copy-start.8 = (s32[1,24]{1,0:T(1,128)S(1)}, s32[1,24]{1,0:T(1,128)}, u32[]{:S(2)}) copy-start(s32[1,24]{1,0:T(1,128)} %refs_8_.1) | copy-start | bytes 292
  1.3 0.7 %copy-start.9 = (s32[1,4]{1,0:T(1,128)S(1)}, s32[1,4]{1,0:T(1,128)}, u32[]{:S(2)}) copy-start(s32[1,4]{1,0:T(1,128)} %refs_10_.1) | copy-start | bytes 52
  2.0 1.1 %copy-start = (bf16[24,128,128]{2,1,0:T(8,128)(2,1)S(1)}, bf16[24,128,128]{2,1,0:T(8,128)(2,1)}, u32[]{:S(2)}) copy-start(bf16[24,128,128]{2,1,0:T(8,128)(2,1)} %refs_3_.1) | copy-start | bytes 2359300
  3.1 1.0 %copy-start.1 = (bf16[512,512]{1,0:T(8,128)(2,1)S(1)}, bf16[512,512]{1,0:T(8,128)(2,1)}, u32[]{:S(2)}) copy-start(bf16[512,512]{1,0:T(8,128)(2,1)} %param.11) | copy-start | bytes 1572868
  4.2 1.0 %copy-start.2 = (bf16[512,512]{1,0:T(8,128)(2,1)S(1)}, bf16[512,512]{1,0:T(8,128)(2,1)}, u32[]{:S(2)}) copy-start(bf16[512,512]{1,0:T(8,128)(2,1)} %refs_1_.1) | copy-start | bytes 1572868
  5.2 1.0 %copy-start.3 = (bf16[512,512]{1,0:T(8,128)(2,1)S(1)}, bf16[512,512]{1,0:T(8,128)(2,1)}, u32[]{:S(2)}) copy-start(bf16[512,512]{1,0:T(8,128)(2,1)} %refs_2_.1) | copy-start | bytes 1572868
  6.2 1.0 %copy-start.4 = (bf16[1,4,128,512]{3,2,1,0:T(8,128)(2,1)S(1)}, bf16[1,4,128,512]{3,2,1,0:T(8,128)(2,1)}, u32[]{:S(2)}) copy-start(bf16[1,4,128,512]{3,2,1,0:T(8,128)(2,1)} %refs_4_.1) | copy-start | bytes 1572868
  7.3 1.0 %copy-start.5 = (bf16[1,4,128,512]{3,2,1,0:T(8,128)(2,1)S(1)}, bf16[1,4,128,512]{3,2,1,0:T(8,128)(2,1)}, u32[]{:S(2)}) copy-start(bf16[1,4,128,512]{3,2,1,0:T(8,128)(2,1)} %refs_5_.1) | copy-start | bytes 1572868

commit v2 on v1

--- a/solution.py
+++ b/solution.py
@@ -66,7 +66,11 @@
         s2send=v((3, piece, width), BF16),
         s2recv=v((3, piece, width), BF16),
         xbuf=v((max(n_extra, 1), 4, piece, width), BF16),
-        gw=v((width, width), BF16),
+        mine=v((piece, width), BF16),
+        mixv=v((1, width), F32),
+        row_s=pltpu.SMEM((1, entries), jnp.int32),
+        src_s=pltpu.SMEM((1, entries), jnp.int32),
+        tile_s=pltpu.SMEM((1, rounds), jnp.int32),
         lsem=pltpu.SemaphoreType.DMA((16,)),
         ssem=pltpu.SemaphoreType.DMA((96,)),
         rsem=pltpu.SemaphoreType.DMA((96,)),
@@ -75,8 +79,9 @@
 
 def kernel(names, nbits, *refs):
     (features, weight, grad_out, adjacency, stale_feat, stale_grad, blend,
-     tile_row, tile_src, tile_count, send_tile, out_hbm, gf_hbm, gw_hbm) = refs[:14]
+     row_hbm, src_hbm, tile_hbm, tile_count, out_any, gf_any, gw_any) = refs[:14]
     s = dict(zip(names, refs[14:]))
+    tile_row, tile_src, send_tile = s["row_s"], s["src_s"], s["tile_s"]
     tiles, block, width = s["feat"].shape
     rounds = s["fsend"].shape[0]
     entries = s["adj"].shape[0]
@@ -97,7 +102,8 @@
 
     loads = {}
     for i, (src, name) in enumerate((
-            (features, "feat"), (adjacency, "adj"), (stale_feat.at[0], "sfeat"),
+            (tile_hbm, "tile_s"), (features, "feat"), (row_hbm, "row_s"), (src_hbm, "src_s"),
+            (adjacency, "adj"), (blend, "mixv"), (stale_feat.at[0], "sfeat"),
             (weight, "wgt"), (grad_out, "gout"), (stale_grad.at[0], "sgrad"))):
         loads[name] = pltpu.make_async_copy(src, s[name], s["lsem"].at[i])
         loads[name].start()
@@ -115,12 +121,15 @@
     for m in sorted(peers):
         pl.semaphore_signal(barrier, inc=1, device_id=(flip(me, m),), device_id_type=MESH)
 
+    loads["tile_s"].wait()
     loads["feat"].wait()
     for r in range(rounds):
         s["fsend"][r] = s["feat"][send_tile[0, r]]
     pl.semaphore_wait(barrier, len(peers))
     fcopies = [remote(s["fsend"].at[r], s["frecv"].at[r], round_mask[r]) for r in range(rounds)]
 
+    for name in ("row_s", "src_s"):
+        loads[name].wait()
     live = tile_count[0]
     cells = tiles + rounds
     keys = [jnp.where(e < live, tile_row[0, e] * cells + tile_src[0, e], -1 - e) for e in range(entries)]
@@ -138,7 +147,8 @@
                 last = jnp.where(keys[e] == t * cells + c, e + 1, last)
             s["dense"][t * block:(t + 1) * block, c * block:(c + 1) * block] = s["chain"][last].astype(BF16)
 
-    mix = blend[...]
+    loads["mixv"].wait()
+    mix = s["mixv"][...]
     keep = 1.0 - mix
     s["part"][...] = jnp.dot(s["dense"][:, :nodes], s["feat"][...].reshape(nodes, width),
                              preferred_element_type=F32)
@@ -158,7 +168,7 @@
         sigma = jax.nn.sigmoid(pre)
         s["outv"][rows, :] = (pre * sigma).astype(BF16)
         s["dpre"][rows, :] = (s["gout"][rows, :].astype(F32) * sigma * (1.0 + pre * (1.0 - sigma))).astype(BF16)
-    out_copy = pltpu.make_async_copy(s["outv"], out_hbm, s["lsem"].at[8])
+    out_copy = pltpu.make_async_copy(s["outv"], out_any, s["lsem"].at[12])
     out_copy.start()
 
     j0 = bit_of(me, 0)
@@ -238,17 +248,20 @@
     arrivals = {}
 
     def forward(kc, kp, kz, level):
-        ref = s["gw"].at[gw_rows(kc, kp, kz)]
+        dst = gw_any.at[gw_rows(kc, kp, kz)]
+        ref = s["mine"] if level > 2 else dst
         if level > 2:
             for k in (3, 2, 1):
-                arrivals[kc, kp, k] = remote(ref, ref, k << 3)
+                arrivals[kc, kp, k] = remote(ref, dst, k << 3)
         if level > 1:
             for k in (3, 1, 2):
-                arrivals[kc, k, kz] = remote(ref, ref, k << 1)
-        arrivals[1, kp, kz] = remote(ref, ref, 1)
-
-    s["gw"][gw_rows(0, 0, 0), :] = total.astype(BF16)
+                arrivals[kc, k, kz] = remote(ref, dst, k << 1)
+        arrivals[1, kp, kz] = remote(ref, dst, 1)
+
+    s["mine"][...] = total.astype(BF16)
     forward(0, 0, 0, 3)
+    own = pltpu.make_async_copy(s["mine"], gw_any.at[gw_rows(0, 0, 0)], s["lsem"].at[14])
+    own.start()
 
     loads["sgrad"].wait()
     hot = [[jnp.where(send_tile[0, r] == t, 1.0, 0.0).astype(F32) for r in range(rounds)] for t in range(tiles)]
@@ -259,7 +272,7 @@
             rows = slice(t * block, (t + 1) * block)
             s["back"][rows, :] = s["back"][rows, :] + hot[t][r] * corrected
     s["gfeat"][...] = s["back"][...].astype(BF16)
-    gf_copy = pltpu.make_async_copy(s["gfeat"], gf_hbm, s["lsem"].at[9])
+    gf_copy = pltpu.make_async_copy(s["gfeat"], gf_any, s["lsem"].at[13])
     gf_copy.start()
 
     for kz in (1, 2, 3):
@@ -272,13 +285,20 @@
     for kz in range(4):
         for kp in range(4):
             arrivals[1, kp, kz].wait_recv()
-    gw_copy = pltpu.make_async_copy(s["gw"], gw_hbm, s["lsem"].at[10])
-    gw_copy.start()
     for c in pending:
         c.wait_send()
+    own.wait()
     out_copy.wait()
     gf_copy.wait()
-    gw_copy.wait()
+
+
+def finish(*refs):
+    ins, outs, sem = refs[:3], refs[3:6], refs[6]
+    copies = [pltpu.make_async_copy(a, b, sem.at[i]) for i, (a, b) in enumerate(zip(ins, outs))]
+    for c in copies:
+        c.start()
+    for c in copies:
+        c.wait()
 
 
 def body(nbits, features, weight, grad_out, adjacency, tile_row, tile_src, tile_count,
@@ -289,23 +309,32 @@
     tiles = nodes // block
     n_extra = (max(nbits - 5, 0) + 1) // 2
     scratch = names_and_shapes(tiles, block, width, entries, rounds, n_extra)
-    hbm = pl.BlockSpec(memory_space=pl.ANY)
-    smem = pl.BlockSpec(memory_space=pltpu.SMEM)
-    vmem = pl.BlockSpec(memory_space=pltpu.VMEM)
-    out, gf, gw = pl.pallas_call(
+    hbm = pl.BlockSpec(memory_space=pltpu.HBM)
+    free = pl.BlockSpec(memory_space=pl.ANY)
+    results = (jax.ShapeDtypeStruct((nodes, width), BF16),
+               jax.ShapeDtypeStruct((nodes, width), BF16),
+               jax.ShapeDtypeStruct((width, width), BF16))
+    found = pl.pallas_call(
         functools.partial(kernel, tuple(scratch), nbits),
         name="layer",
-        out_shape=(jax.ShapeDtypeStruct((nodes, width), BF16),
-                   jax.ShapeDtypeStruct((nodes, width), BF16),
-                   jax.ShapeDtypeStruct((width, width), BF16)),
-        in_specs=[hbm] * 6 + [vmem] + [smem] * 4,
-        out_specs=(hbm, hbm, hbm),
+        out_shape=results,
+        in_specs=[hbm] * 10 + [pl.BlockSpec(memory_space=pltpu.SMEM)],
+        out_specs=(free,) * 3,
         scratch_shapes=list(scratch.values()),
         compiler_params=pltpu.CompilerParams(collective_id=0, has_side_effects=True,
                                              vmem_limit_bytes=48 * 1024 * 1024),
-    )(features.reshape(tiles, block, width), weight, grad_out, adjacency, stale_feat, stale_grad,
-      blend.reshape(1, width), tile_row, tile_src, tile_count, send_tile)
-    return out, gf, gw
+    )(*(pltpu.with_memory_space_constraint(x, pltpu.HBM) for x in (
+        features.reshape(tiles, block, width), weight, grad_out, adjacency, stale_feat, stale_grad,
+        blend.reshape(1, width), tile_row, tile_src, send_tile)), tile_count)
+    return tuple(pl.pallas_call(
+        finish,
+        name="finish",
+        out_shape=results,
+        in_specs=[free] * 3,
+        out_specs=(hbm,) * 3,
+        scratch_shapes=[pltpu.SemaphoreType.DMA((3,))],
+        compiler_params=pltpu.CompilerParams(vmem_limit_bytes=16 * 1024 * 1024),
+    )(*found))
 
 
 def solution(mesh):

time: 42 us -> 32.7 us (0.78)
  local copies, waits for them, and re-layouts: 9.39 us -> 0 us
    unnamed x23 -> x0, local copies, waits for them, and re-layouts: 9.39 us -> none
    pallas_call x0 -> x1, Pallas kernels: none -> 1.17 us  [body(): pl.pallas_call(finish, name='finish', out_shape=results, in_specs=[free]...]
    pallas_call x1, Pallas kernels: 30.9 us -> 30.1 us  [body(): pl.pallas_call(functools.partial(kernel, tuple(scratch), nbits), name='la...]
where the time goes in v2:
time: 32.7 us; the launch traced here: 32.5 us
  Pallas kernels  31.3 us (96%)
  between operations  1.29 us (4%)
    pallas_call x1, Pallas kernels, body(): pl.pallas_call(functools.partial(kernel, tuple(scratch), nbits), name='la...  30.1 us
    pallas_call x1, Pallas kernels, body(): pl.pallas_call(finish, name='finish', out_shape=results, in_specs=[free]...  1.17 us

profile of v2, /device:TPU:0, one launch (start us, length us, event | category | flops | bytes accessed | tf_op | source)
XLA Modules:
  0.0 32.5 jit_solution(11572256645236103637)
XLA Ops:
  1.3 30.1 %layer.1 = (bf16[512,512]{1,0:T(8,128)(2,1)S(1)}, bf16[512,512]{1,0:T(8,128)(2,1)S(1)}, bf16[512,512]{1,0:T(8,128)(2,1)S(1)}) custom-call(bf16[4,128,512]{2,1,0:T(8,128)(2,1)} %bitcast.2, bf16[512,512]{1,0:T(8,128)(2,1)} %refs_1_.1, bf16[512,512]{1,0:T(8,128)(2,1)} %refs_2_.1, bf16[24,128,128]{2,1,0:T(8,128)(2,1)} %refs_3_.1, ...), custom_call_target="tpu_custom_call" | custom-call | tf_op jit(solution)/shard_map/layer/pallas_call | solution.py:317
  31.4 1.2 %finish.1 = (bf16[512,512]{1,0:T(8,128)(2,1)}, bf16[512,512]{1,0:T(8,128)(2,1)}, bf16[512,512]{1,0:T(8,128)(2,1)}) custom-call(bf16[512,512]{1,0:T(8,128)(2,1)S(1)} %get-tuple-element.6.refs_0_, bf16[512,512]{1,0:T(8,128)(2,1)S(1)} %get-tuple-element.7.refs_1_, bf16[512,512]{1,0:T(8,128)(2,1)S(1)} %get-tuple-element.8.refs_2_), custom_call_target="tpu_custom_call" | custom-call | tf_op jit(solution)/shard_map/finish/pallas_call | solution.py:329

commit v3 on v2

--- a/solution.py
+++ b/solution.py
@@ -198,11 +198,13 @@
         total = s["acc"][quarter_rows(k), :] + s["s0recv"][quarter_rows(k), :].astype(F32)
         if k == 0:
             s["acc"][quarter_rows(0), :] = total
-            continue
-        s["s1send"][quarter_rows(k), :] = total.astype(BF16)
-        for kz in (3, 2, 1, 0):
-            plane[k, kz] = remote(s["s1send"].at[piece_rows(kz, flip(j1, k) * quarter)],
-                                  s["s1recv"].at[k - 1, piece_rows(kz)], k << 1)
+        else:
+            s["s1send"][quarter_rows(k), :] = total.astype(BF16)
+        if k == order1[2]:
+            for kz in (3, 2, 1, 0):
+                for kp in order1[:3]:
+                    plane[kp, kz] = remote(s["s1send"].at[piece_rows(kz, flip(j1, kp) * quarter)],
+                                           s["s1recv"].at[kp - 1, piece_rows(kz)], kp << 1)
 
     s["dagg"][...] = lax.dot_general(s["dpre"][...], s["wgt"][...], (((1,), (1,)), ((), ())),
                                      preferred_element_type=F32).astype(BF16)
@@ -227,6 +229,20 @@
             line[kz] = remote(s["s2send"].at[kz - 1], s["s2recv"].at[kz - 1], kz << 3)
     for r in late:
         gcopies[r] = remote(s["gsend"].at[r], s["grecv"].at[r], round_mask[r])
+    loads["sgrad"].wait()
+    hot = [[jnp.where(send_tile[0, r] == t, 1.0, 0.0).astype(F32) for r in range(rounds)] for t in range(tiles)]
+
+    def mix_rounds(which, dst):
+        for r in which:
+            gcopies[r].wait_recv()
+        for t in range(tiles):
+            rows = slice(t * block, (t + 1) * block)
+            acc = s["back"][rows, :]
+            for r in which:
+                acc = acc + hot[t][r] * (keep * s["sgrad"][r].astype(F32) + mix * s["grecv"][r].astype(F32))
+            s[dst][rows, :] = acc.astype(s[dst].dtype)
+
+    mix_rounds([r for r in range(rounds) if r not in late], "back")
     for kz in (1, 2, 3):
         line[kz].wait_recv()
         total = total + s["s2recv"][kz - 1].astype(F32)
@@ -263,15 +279,7 @@
     own = pltpu.make_async_copy(s["mine"], gw_any.at[gw_rows(0, 0, 0)], s["lsem"].at[14])
     own.start()
 
-    loads["sgrad"].wait()
-    hot = [[jnp.where(send_tile[0, r] == t, 1.0, 0.0).astype(F32) for r in range(rounds)] for t in range(tiles)]
-    for r in range(rounds):
-        gcopies[r].wait_recv()
-        corrected = keep * s["sgrad"][r].astype(F32) + mix * s["grecv"][r].astype(F32)
-        for t in range(tiles):
-            rows = slice(t * block, (t + 1) * block)
-            s["back"][rows, :] = s["back"][rows, :] + hot[t][r] * corrected
-    s["gfeat"][...] = s["back"][...].astype(BF16)
+    mix_rounds(late, "gfeat")
     gf_copy = pltpu.make_async_copy(s["gfeat"], gf_any, s["lsem"].at[13])
     gf_copy.start()
 
@@ -294,7 +302,13 @@
 
 def finish(*refs):
     ins, outs, sem = refs[:3], refs[3:6], refs[6]
-    copies = [pltpu.make_async_copy(a, b, sem.at[i]) for i, (a, b) in enumerate(zip(ins, outs))]
+    parts = 4
+    copies = []
+    for i, (a, b) in enumerate(zip(ins, outs)):
+        step = a.shape[0] // parts
+        for q in range(parts):
+            rows = pl.ds(q * step, step)
+            copies.append(pltpu.make_async_copy(a.at[rows], b.at[rows], sem.at[i * parts + q]))
     for c in copies:
         c.start()
     for c in copies:
@@ -332,7 +346,7 @@
         out_shape=results,
         in_specs=[free] * 3,
         out_specs=(hbm,) * 3,
-        scratch_shapes=[pltpu.SemaphoreType.DMA((3,))],
+        scratch_shapes=[pltpu.SemaphoreType.DMA((12,))],
         compiler_params=pltpu.CompilerParams(vmem_limit_bytes=16 * 1024 * 1024),
     )(*found))
 

time: 32.7 us -> 32.8 us (level)
  no operation moved by 1% of the time
where the time goes in v3:
time: 32.8 us; the launch traced here: 32.7 us
  Pallas kernels  31.4 us (96%)
  between operations  1.29 us (4%)
    pallas_call x1, Pallas kernels, body(): pl.pallas_call(functools.partial(kernel, tuple(scratch), nbits), name='la...  30.2 us
    pallas_call x1, Pallas kernels, body(): pl.pallas_call(finish, name='finish', out_shape=results, in_specs=[free]...  1.24 us

profile of v3, /device:TPU:0, one launch (start us, length us, event | category | flops | bytes accessed | tf_op | source)
XLA Modules:
  0.0 32.7 jit_solution(17157852227830260538)
XLA Ops:
  1.3 30.2 %layer.1 = (bf16[512,512]{1,0:T(8,128)(2,1)S(1)}, bf16[512,512]{1,0:T(8,128)(2,1)S(1)}, bf16[512,512]{1,0:T(8,128)(2,1)S(1)}) custom-call(bf16[4,128,512]{2,1,0:T(8,128)(2,1)} %bitcast.2, bf16[512,512]{1,0:T(8,128)(2,1)} %refs_1_.1, bf16[512,512]{1,0:T(8,128)(2,1)} %refs_2_.1, bf16[24,128,128]{2,1,0:T(8,128)(2,1)} %refs_3_.1, ...), custom_call_target="tpu_custom_call" | custom-call | tf_op jit(solution)/shard_map/layer/pallas_call | solution.py:331
  31.4 1.2 %finish.1 = (bf16[512,512]{1,0:T(8,128)(2,1)}, bf16[512,512]{1,0:T(8,128)(2,1)}, bf16[512,512]{1,0:T(8,128)(2,1)}) custom-call(bf16[512,512]{1,0:T(8,128)(2,1)S(1)} %get-tuple-element.6.refs_0_, bf16[512,512]{1,0:T(8,128)(2,1)S(1)} %get-tuple-element.7.refs_1_, bf16[512,512]{1,0:T(8,128)(2,1)S(1)} %get-tuple-element.8.refs_2_), custom_call_target="tpu_custom_call" | custom-call | tf_op jit(solution)/shard_map/finish/pallas_call | solution.py:343

commit v4 on v3

--- a/solution.py
+++ b/solution.py
@@ -212,9 +212,8 @@
                                       preferred_element_type=F32).astype(BF16).reshape(rounds, block, width)
     gcopies = {}
     late = [r for r in range(rounds) if round_mask[r] in (2, 4)]
-    for r in range(rounds):
-        if r not in late:
-            gcopies[r] = remote(s["gsend"].at[r], s["grecv"].at[r], round_mask[r])
+    for r in [r for r in range(rounds) if r not in late] + late:
+        gcopies[r] = remote(s["gsend"].at[r], s["grecv"].at[r], round_mask[r])
     s["back"][...] = lax.dot_general(s["dense"][:, :nodes], s["dagg"][...], (((0,), (0,)), ((), ())),
                                      preferred_element_type=F32)
 
@@ -227,8 +226,6 @@
         if kz:
             s["s2send"][kz - 1] = total.astype(BF16)
             line[kz] = remote(s["s2send"].at[kz - 1], s["s2recv"].at[kz - 1], kz << 3)
-    for r in late:
-        gcopies[r] = remote(s["gsend"].at[r], s["grecv"].at[r], round_mask[r])
     loads["sgrad"].wait()
     hot = [[jnp.where(send_tile[0, r] == t, 1.0, 0.0).astype(F32) for r in range(rounds)] for t in range(tiles)]
 
@@ -302,7 +299,7 @@
 
 def finish(*refs):
     ins, outs, sem = refs[:3], refs[3:6], refs[6]
-    parts = 4
+    parts = 1
     copies = []
     for i, (a, b) in enumerate(zip(ins, outs)):
         step = a.shape[0] // parts
@@ -346,7 +343,7 @@
         out_shape=results,
         in_specs=[free] * 3,
         out_specs=(hbm,) * 3,
-        scratch_shapes=[pltpu.SemaphoreType.DMA((12,))],
+        scratch_shapes=[pltpu.SemaphoreType.DMA((3,))],
         compiler_params=pltpu.CompilerParams(vmem_limit_bytes=16 * 1024 * 1024),
     )(*found))
 

time: 32.8 us -> 32.2 us (0.982)
  Pallas kernels: 31.4 us -> 30.8 us
    pallas_call x1, Pallas kernels: 30.2 us -> 29.6 us  [body(): pl.pallas_call(functools.partial(kernel, tuple(scratch), nbits), name='la...]
where the time goes in v4:
time: 32.2 us; the launch traced here: 32.1 us
  Pallas kernels  30.8 us (96%)
  between operations  1.29 us (4%)
    pallas_call x1, Pallas kernels, body(): pl.pallas_call(functools.partial(kernel, tuple(scratch), nbits), name='la...  29.6 us
    pallas_call x1, Pallas kernels, body(): pl.pallas_call(finish, name='finish', out_shape=results, in_specs=[free]...  1.17 us

profile of v4, /device:TPU:0, one launch (start us, length us, event | category | flops | bytes accessed | tf_op | source)
XLA Modules:
  0.0 32.1 jit_solution(3688816447738086541)
XLA Ops:
  1.3 29.6 %layer.1 = (bf16[512,512]{1,0:T(8,128)(2,1)S(1)}, bf16[512,512]{1,0:T(8,128)(2,1)S(1)}, bf16[512,512]{1,0:T(8,128)(2,1)S(1)}) custom-call(bf16[4,128,512]{2,1,0:T(8,128)(2,1)} %bitcast.2, bf16[512,512]{1,0:T(8,128)(2,1)} %refs_1_.1, bf16[512,512]{1,0:T(8,128)(2,1)} %refs_2_.1, bf16[24,128,128]{2,1,0:T(8,128)(2,1)} %refs_3_.1, ...), custom_call_target="tpu_custom_call" | custom-call | tf_op jit(solution)/shard_map/layer/pallas_call | solution.py:328
  30.9 1.2 %finish.1 = (bf16[512,512]{1,0:T(8,128)(2,1)}, bf16[512,512]{1,0:T(8,128)(2,1)}, bf16[512,512]{1,0:T(8,128)(2,1)}) custom-call(bf16[512,512]{1,0:T(8,128)(2,1)S(1)} %get-tuple-element.6.refs_0_, bf16[512,512]{1,0:T(8,128)(2,1)S(1)} %get-tuple-element.7.refs_1_, bf16[512,512]{1,0:T(8,128)(2,1)S(1)} %get-tuple-element.8.refs_2_), custom_call_target="tpu_custom_call" | custom-call | tf_op jit(solution)/shard_map/finish/pallas_call | solution.py:340
